TPU v7x, 32 devices: a whole 2x2x4 slice. The times are simulated.
32 devices in a mesh: sky: 8 (over z, y), band: 4 (over x, core).
Axes of the slice: x: 2, y: 2, z: 4, core: 2. Of those that a mesh axis runs over, the one named last changes fastest.
Arguments:
- exposures: bfloat16 [8, 4, 1024, 1024], P('sky', 'band'), may hold values from -6 to 6
- inv_variance: bfloat16 [8, 4, 1024, 1024], P('sky', 'band'), may hold values from 0.25 to 4
- mask_planes: int32 [8, 4, 2, 35], P('sky', 'band'), may hold values from 0 to 1073741823, as said below
- sky_columns: int32 [8, 4, 8], replicated, may hold values from 0 to 7, as said below
- basis_rows: float32 [9, 25], replicated, may hold values from -1 to 1
- basis_cols: float32 [9, 25], replicated, may hold values from -1 to 1
- match_coeffs: float32 [8, 4, 9], P('sky', 'band'), may hold values from -2 to 2
- detect_taps: float32 [4, 31], P('band'), may hold values from 0.05 to 0.3
Outputs:
- difference: bfloat16 [8, 4, 1024, 1024], P('sky', 'band')
- detection: float32 [1024, 1024], P('band', 'sky')
Inputs may be any that keep to these rules, and one draw needn't show every extreme that they name: Each row sky_columns[e, b] holds 8 consecutive sky tile columns in order, counted modulo 8; every sky tile column is covered by some exposure of every band. Bit j of mask_planes[e, b, 0, w] marks pixel column 30 w + j of that exposure as bad and bit j of mask_planes[e, b, 1, w] pixel row 30 w + j; bits past 1024 are ignored. In every draw some word has all 30 bits set.
All inputs are finite; a program needn't handle non-finite values.
Results may differ from a plain program's by a relative error of at most 0.0095.
Values may be sent and summed in bfloat16 or wider, within the bound.
No kernel may reach another device: no remote copies, remote signals or barrier semaphores. Data moves between devices by JAX's collectives and lax.ppermute only.
A program may use at most 128 MiB of HBM per device.

v0:
```python
import jax
import jax.numpy as jnp
from jax import lax
from jax.sharding import PartitionSpec as P

TILE = 128
NB = 9
TAPS = 25
DTAPS = 31


def with_halo(block, sides, width):
    for axis, dim in sides:
        count = lax.axis_size(axis)
        forward = [(i, i + 1) for i in range(count - 1)]
        forward.append((count - 1, 0))
        backward = [(target, source) for source, target in forward]
        low = lax.ppermute(
            lax.slice_in_dim(block, block.shape[dim] - width, None, axis=dim), axis, forward
        )
        high = lax.ppermute(lax.slice_in_dim(block, 0, width, axis=dim), axis, backward)
        block = jnp.concatenate([low, block, high], axis=dim)
    return block


def band_matrix(tap_rows, window_width):
    offsets = (
        jnp.arange(window_width, dtype=jnp.int32)[:, None]
        - jnp.arange(TILE, dtype=jnp.int32)[None, :]
    )
    selector = (
        offsets[:, :, None] == jnp.arange(tap_rows.shape[1], dtype=jnp.int32)[None, None, :]
    ).astype(jnp.float32)
    return jnp.einsum(
        "wtl,kl->kwt", selector, tap_rows.astype(jnp.float32), precision=lax.Precision.HIGHEST
    ).astype(jnp.bfloat16)


def keep_pixels(planes, side_length):
    places = jnp.arange(side_length, dtype=jnp.int32)
    column_bits = jnp.bitwise_and(jnp.right_shift(planes[0][places // 30], places % 30), 1)
    row_bits = jnp.bitwise_and(jnp.right_shift(planes[1][places // 30], places % 30), 1)
    return jnp.logical_and(row_bits[:, None] == 0, column_bits[None, :] == 0)


def psf_match(picture, column_taps, row_taps):
    side_length = picture.shape[1]
    block_count = side_length // TILE
    margin = TAPS // 2
    width_full = TILE + 2 * margin
    padded = jnp.pad(picture, ((0, 0), (margin, margin)))
    blocks = jnp.stack(
        [
            padded[:, TILE * block_index : TILE * block_index + width_full]
            for block_index in range(block_count)
        ],
        0,
    )
    column_band = band_matrix(column_taps, width_full)
    column_pass = jnp.einsum(
        "jyw,kwt->kyjt", blocks, column_band, preferred_element_type=jnp.float32
    )
    column_pass = column_pass.reshape(NB, side_length, side_length).astype(jnp.bfloat16)
    row_padded = jnp.pad(column_pass, ((0, 0), (margin, margin), (0, 0)))
    row_blocks = jnp.stack(
        [
            row_padded[:, TILE * block_index : TILE * block_index + width_full, :]
            for block_index in range(block_count)
        ],
        0,
    )
    row_band = band_matrix(row_taps, width_full)
    summed = jnp.einsum("ikwx,kwt->itx", row_blocks, row_band, preferred_element_type=jnp.float32)
    return summed.reshape(side_length, side_length).astype(jnp.bfloat16)


def average_pieces(pieces):
    matched_in, weight_in = pieces
    weight_float = weight_in.astype(jnp.float32)
    numer = jnp.sum(weight_float * matched_in.astype(jnp.float32), axis=1)
    denom = jnp.sum(weight_float, axis=1)
    return (numer / jnp.maximum(denom, 1.0)).astype(jnp.bfloat16)


def subtract_template(template, matched, own_columns, side_length, sky_count):
    gathered = lax.all_gather(template, "sky", axis=1, tiled=True).reshape(
        side_length, sky_count, TILE
    )
    picked = jnp.take(gathered, own_columns, axis=1).reshape(side_length, side_length)
    return (matched.astype(jnp.float32) - picked.astype(jnp.float32)).astype(jnp.bfloat16)


def body(
    exposures,
    inv_variance,
    mask_planes,
    sky_columns,
    basis_rows,
    basis_cols,
    match_coeffs,
    detect_taps,
):
    picture = exposures[0, 0]
    side_length = picture.shape[0]
    block_count = side_length // TILE
    sky_count = lax.axis_size("sky")
    own_sky = lax.axis_index("sky")
    own_band = lax.axis_index("band")
    column_taps = (match_coeffs[0, 0][:, None] * basis_cols).astype(jnp.bfloat16)
    matched = psf_match(picture, column_taps, basis_rows.astype(jnp.bfloat16))
    keep = keep_pixels(mask_planes[0, 0], side_length)
    variance_inv = inv_variance[0, 0]
    weight = jnp.where(keep, variance_inv, jnp.zeros_like(variance_inv))
    own_columns = sky_columns[own_sky, own_band]
    empty_slots = jnp.zeros((side_length, sky_count, TILE), jnp.bfloat16)
    send_matched = empty_slots.at[:, own_columns, :].set(
        matched.reshape(side_length, block_count, TILE)
    )
    send_weight = empty_slots.at[:, own_columns, :].set(
        weight.reshape(side_length, block_count, TILE)
    )
    template = average_pieces(
        (
            lax.all_to_all(send_matched, "sky", split_axis=1, concat_axis=1, tiled=True),
            lax.all_to_all(send_weight, "sky", split_axis=1, concat_axis=1, tiled=True),
        )
    )
    difference = subtract_template(template, matched, own_columns, side_length, sky_count)
    margin = DTAPS // 2
    width_full = TILE + 2 * margin
    filter_band = band_matrix(detect_taps.astype(jnp.bfloat16), width_full)[0]
    widened = with_halo(template, (("sky", 1),), margin)
    smoothed = jnp.dot(widened, filter_band, preferred_element_type=jnp.float32).astype(
        jnp.bfloat16
    )
    smooth_padded = jnp.pad(smoothed, ((margin, margin), (0, 0)))
    smooth_blocks = jnp.stack(
        [
            smooth_padded[TILE * block_index : TILE * block_index + width_full]
            for block_index in range(block_count)
        ],
        0,
    )
    filtered = jnp.einsum(
        "iwx,wt->itx", smooth_blocks, filter_band, preferred_element_type=jnp.float32
    ).reshape(side_length, TILE)
    power = filtered * filtered
    detection = lax.psum_scatter(power, "band", scatter_dimension=0, tiled=True)
    return (difference[None, None], detection)


def solution(mesh):
    in_specs = (
        P("sky", "band", None, None),
        P("sky", "band", None, None),
        P("sky", "band", None, None),
        P(),
        P(),
        P(),
        P("sky", "band", None),
        P("band", None),
    )
    out_specs = (P("sky", "band", None, None), P("band", "sky"))
    return jax.shard_map(body, mesh=mesh, in_specs=in_specs, out_specs=out_specs, check_vma=False)
```

profile of v0, /device:TPU:0, one launch (start us, length us, event | category | flops | bytes accessed | tf_op | source)
XLA Modules:
  0.0 304.6 jit_solution(1016820240146248366)
XLA Ops:
  8.0 2.9 copy.65
  11.0 0.1 fusion.40
  11.1 0.1 fusion.39
  11.2 0.1 fusion.38
  11.2 0.1 fusion.37
  11.3 0.1 fusion.36
  11.4 0.1 fusion.35
  11.5 0.1 fusion.34
  11.6 0.3 copy-done.3
  11.8 0.6 fusion.19
  12.4 9.2 %convolution_convert_fusion = bf16[9,128,8,1024]{3,1,2,0:T(8,128)(2,1)} fusion(bf16[8,1024,152]{1,2,0:T(8,128)(2,1)S(1)} %fusion.34, bf16[9,152,128,1]{2,0,1,3:T(8,128)(2,1)S(1)} %fusion.19), kind=kOutput, calls=%fused_computation.5 | convolution fusion | flops 2878341120 | bytes 21714944 | tf_op jit(solution)/shard_map/jyw,kwt->kyjt/dot_general | solution.py:60
  21.6 24.6 %copy.67 = bf16[9,1024,1024]{2,1,0:T(8,128)(2,1)} copy(bf16[9,1024,1024]{1,2,0:T(8,128)(2,1)} %bitcast.237) | data formatting | bytes 37748736 | tf_op jit(solution)/shard_map/convert_element_type | solution.py:63
  46.3 4.3 %fusion.2 = bf16[8,9,152,1024]{3,2,1,0:T(8,128)(2,1)} fusion(bf16[9,1024,1024]{2,1,0:T(8,128)(2,1)} %copy.67), kind=kLoop, calls=%fused_computation.13 | loop fusion | bytes 21676032
  50.6 3.8 %copy-done = bf16[9,1024,1024]{2,1,0:T(8,128)(2,1)S(1)} copy-done((bf16[9,1024,1024]{2,1,0:T(8,128)(2,1)S(1)}, bf16[9,1024,1024]{2,1,0:T(8,128)(2,1)}, u32[]{:S(2)}) %copy-start) | copy-done | bytes 18874392
  54.4 2.5 fusion.10
  56.9 2.4 fusion.9
  59.3 2.5 fusion.8
  61.8 2.5 fusion.7
  64.3 2.4 fusion.6
  66.7 2.4 fusion.5
  69.2 2.4 fusion.4
  71.6 0.6 fusion.20
  72.2 9.9 %bitcast_convert_fusion = bf16[128,8,1024]{2,0,1:T(8,128)(2,1)S(1)} fusion(bf16[8,9,152,1024]{3,2,1,0:T(8,128)(2,1)} %fusion.4, bf16[9,152,128]{2,0,1:T(8,128)(2,1)S(1)} %fusion.20), kind=kOutput, calls=%fused_computation.9 | convolution fusion | flops 2869952512 | bytes 24860672 | tf_op jit(solution)/shard_map/ikwx,kwt->itx/dot_general | solution.py:73
  82.1 0.6 copy.89
  82.7 1.7 copy.104
  84.4 0.7 fusion.61
  85.1 1.6 broadcast_in_dim.16.clone.1
  86.7 5.7 %scatter_fusion.1 = bf16[1024,8,128]{2,0,1:T(8,128)(2,1)} fusion(bf16[1024,8,128]{2,0,1:T(8,128)(2,1)} %broadcast_in_dim.16.clone.1, s32[8]{0:T(128)S(1)} %fusion.61, bf16[8,1024,128]{2,1,0:T(8,128)(2,1)} %bitcast.248), kind=kCustom, calls=%fused_computation.2 | custom fusion | bytes 6291488 | tf_op jit(solution)/shard_map/scatter | solution.py:116
  92.4 7.3 %all-to-all-start.1 = ((bf16[1024,8,128]{2,0,1:T(8,128)(2,1)}), bf16[1024,8,128]{2,0,1:T(8,128)(2,1)}, u32[]{:S(2)}, u32[]{:S(2)}) async-start(bf16[1024,8,128]{2,0,1:T(8,128)(2,1)} %scatter_fusion.1), calls=%async_computation.1 | async-start | bytes 4194304 | tf_op jit(solution)/shard_map/all_to_all | solution.py:124
  99.8 3.9 %copy.75 = bf16[1,1,1024,1024]{2,3,1,0:T(8,128)(2,1)} copy(bf16[1,1,1024,1024]{3,2,1,0:T(8,128)(2,1)} %param.9) | data formatting | bytes 4194304 | tf_op args[1]
  103.7 3.9 %copy.76 = bf16[1024,8,128]{2,0,1:T(8,128)(2,1)} copy(bf16[1024,8,128]{0,2,1:T(8,128)(2,1)} %bitcast.253) | data formatting | bytes 4194304 | tf_op jit(solution)/shard_map/squeeze | solution.py:112
  108.8 0.7 fusion.67
  109.5 0.7 fusion.64
  110.2 4.6 %compare_select_fusion.2 = s32[1024,1]{0,1:T(1,128)S(1)} fusion(s32[]{:T(128)} %bitcast.99, s32[]{:T(128)} %bitcast.100, s32[]{:T(128)} %bitcast.101, s32[]{:T(128)} %bitcast.102, s32[]{:T(128)} %bitcast.103, s32[]{:T(128)} %bitcast.105, s32[]{:T(128)} %bitcast.104), kind=kLoop, calls=%fused_computation.125 | loop fusion | flops 23552 | bytes 4124 | tf_op jit(solution)/shard_map/gather | solution.py:41
  114.8 0.7 fusion.65
  115.5 0.7 fusion.66
  116.3 4.4 %compare_select_fusion.1 = s32[1024,1]{0,1:T(1,128)S(1)} fusion(s32[]{:T(128)} %bitcast.63, s32[]{:T(128)} %bitcast.64, s32[]{:T(128)} %bitcast.65, s32[]{:T(128)} %bitcast.66, s32[]{:T(128)} %bitcast.67, s32[]{:T(128)} %bitcast.69, s32[]{:T(128)} %bitcast.68), kind=kLoop, calls=%fused_computation.124 | loop fusion | flops 23552 | bytes 4124 | tf_op jit(solution)/shard_map/gather | solution.py:42
  120.6 17.6 %fusion.49 = pred[8,128]{1,0:T(8,128)(4,1)S(1)} fusion(pred[1024]{0:T(1024)(128)(4,1)S(1)} %compare_reduce_fusion, pred[1024]{0:T(1024)(128)(4,1)S(1)} %compare_reduce_fusion.1, pred[1024]{0:T(1024)(128)(4,1)S(1)} %compare_reduce_fusion.2, pred[1024]{0:T(1024)(128)(4,1)S(1)} %compare_reduce_fusion.3, pred[1024]{0:T(1024)(128)(4,1)S(1)} %compare_reduce_fusion.4, ...), kind=kLoop, calls=%fused_computation.147 | loop fusion | flops 39936 | bytes 33904 | tf_op jit(solution)/shard_map/eq | solution.py:43
  138.3 17.6 %fusion.46 = pred[1024]{0:T(1024)(128)(4,1)S(1)} fusion(pred[1024]{0:T(1024)(128)(4,1)S(1)} %compare_reduce_fusion, pred[1024]{0:T(1024)(128)(4,1)S(1)} %compare_reduce_fusion.1, pred[1024]{0:T(1024)(128)(4,1)S(1)} %compare_reduce_fusion.2, pred[1024]{0:T(1024)(128)(4,1)S(1)} %compare_reduce_fusion.3, pred[1024]{0:T(1024)(128)(4,1)S(1)} %compare_reduce_fusion.4, ...), kind=kLoop, calls=%fused_computation.144 | loop fusion | flops 37888 | bytes 33904 | tf_op jit(solution)/shard_map/eq | solution.py:43
  155.9 3.6 %fusion.16 = bf16[8,1024,128]{2,1,0:T(8,128)(2,1)} fusion(bf16[1024,8,128]{2,0,1:T(8,128)(2,1)} %copy.76, pred[8,128]{1,0:T(8,128)(4,1)S(1)} %fusion.49, pred[1024]{0:T(1024)(128)(4,1)S(1)} %fusion.46), kind=kLoop, calls=%fused_computation.35 | loop fusion | flops 2097152 | bytes 4196352 | tf_op jit(solution)/shard_map/jit(_where)/select_n | solution.py:113
  159.5 1.6 broadcast_in_dim.16.clone
  161.1 5.7 %scatter_fusion = bf16[1024,8,128]{2,0,1:T(8,128)(2,1)} fusion(bf16[1024,8,128]{2,0,1:T(8,128)(2,1)} %broadcast_in_dim.16.clone, s32[8]{0:T(128)S(1)} %fusion.61, bf16[8,1024,128]{2,1,0:T(8,128)(2,1)} %fusion.16), kind=kCustom, calls=%fused_computation.1 | custom fusion | bytes 6291488 | tf_op jit(solution)/shard_map/scatter | solution.py:119
  166.8 53.7 %all_to_all.10 = bf16[1024,8,128]{2,0,1:T(8,128)(2,1)S(1)} all-to-all(bf16[1024,8,128]{2,0,1:T(8,128)(2,1)} %scatter_fusion), channel_id=1, replica_groups=mesh['sky'=8,'band'=4] {'sky'}, dimensions={1} | all-to-all | bytes 4194304 | tf_op jit(solution)/shard_map/all_to_all | solution.py:125
  220.5 2.5 convert_reduce_fusion
  223.0 0.8 divide_convert_fusion
  223.8 0.3 iota_compare_fusion
  224.2 1.2 fusion.63
  225.3 1.5 collective-permute-start
  226.9 3.3 %collective-permute-start.1 = (bf16[1024,15]{1,0:T(8,128)(2,1)S(1)}, bf16[1024,15]{1,0:T(8,128)(2,1)S(1)}, u32[]{:S(2)}, u32[]{:S(2)}) collective-permute-start(bf16[1024,15]{1,0:T(8,128)(2,1)S(1)} %get-tuple-element.11), channel_id=1, source_target_pairs={{4,0},{8,4},{12,8},{16,12},{20,16},{24,20},{28,24},{0,28},{5,1},{9... | collective-permute-start | bytes 92168 | tf_op jit(solution)/shard_map/ppermute | solution.py:21
  230.1 0.5 fusion.11
  230.7 9.0 %collective-permute-done = bf16[1024,15]{1,0:T(8,128)(2,1)S(1)} collective-permute-done((bf16[1024,15]{1,0:T(8,128)(2,1)S(1)}, bf16[1024,15]{1,0:T(8,128)(2,1)S(1)}, u32[]{:S(2)}, u32[]{:S(2)}) %collective-permute-start) | collective-permute-done | bytes 30752 | tf_op jit(solution)/shard_map/ppermute | solution.py:18
  239.6 2.2 collective-permute-done.1
  241.8 0.4 convolution_convert_fusion.1
  242.5 1.1 convolution_multiply_fusion
  243.6 3.2 %copy.81 = f32[1,1,1024,1024]{2,3,1,0:T(8,128)} copy(bf16[1,1,1024,1024]{3,2,1,0:T(8,128)(2,1)S(1)} %bitcast.247) | data formatting | bytes 6291456 | tf_op jit(solution)/shard_map/convert_element_type | solution.py:90
  246.8 0.7 compare_and_fusion
  247.5 0.1 broadcast_bitcast_fusion
  247.6 29.6 %all-gather.2.cloned.1.call-done = bf16[1024,1024]{1,0:T(8,128)(2,1)} async-done(((bf16[1024,128]{1,0:T(8,128)(2,1)}), bf16[1024,1024]{1,0:T(8,128)(2,1)}) %all-gather.2.cloned.1.call-update) | async-done | bytes 2097168 | tf_op jit(solution)/shard_map/all_gather | solution.py:86
  277.1 3.9 %copy.78 = bf16[1024,1024]{0,1:T(8,128)(2,1)} copy(bf16[1024,1024]{1,0:T(8,128)(2,1)} %all-gather.2.cloned.1.call-done) | data formatting | bytes 4194304 | tf_op jit(solution)/shard_map/all_gather | solution.py:86
  281.1 3.0 copy.79
  284.1 2.1 gather_fusion
  286.2 2.9 copy.80
  289.1 4.1 %subtract_convert_fusion = bf16[1,1,1024,1024]{2,3,1,0:T(8,128)(2,1)} fusion(f32[1,1,1024,1024]{2,3,1,0:T(8,128)} %copy.81, bf16[1,1,1024,1024]{2,3,1,0:T(8,128)(2,1)S(1)} %bitcast.249, pred[1024]{0:T(1024)(128)(4,1)S(1)} %broadcast_bitcast_fusion), kind=kLoop, calls=%fused_computation.10 | loop fusion | flops 4194304 | bytes 8389632 | tf_op jit(solution)/shard_map/convert_element_type | solution.py:90
  293.2 3.9 %copy.82 = bf16[1,1,1024,1024]{3,2,1,0:T(8,128)(2,1)} copy(bf16[1,1,1024,1024]{2,3,1,0:T(8,128)(2,1)} %subtract_convert_fusion) | data formatting | bytes 4194304
  (58 shorter events, 1.5 us)
Async XLA Ops:
  11.1 0.7 copy-start.3
  11.1 0.7 copy-start.4
  46.3 8.2 %copy-start = (bf16[9,1024,1024]{2,1,0:T(8,128)(2,1)S(1)}, bf16[9,1024,1024]{2,1,0:T(8,128)(2,1)}, u32[]{:S(2)}) copy-start(bf16[9,1024,1024]{2,1,0:T(8,128)(2,1)} %copy.67) | copy-start | bytes 56623108
  69.2 2.4 copy-start.5
  92.4 74.4 %all-to-all-start.1 = ((bf16[1024,8,128]{2,0,1:T(8,128)(2,1)}), bf16[1024,8,128]{2,0,1:T(8,128)(2,1)}, u32[]{:S(2)}, u32[]{:S(2)}) async-start(bf16[1024,8,128]{2,0,1:T(8,128)(2,1)} %scatter_fusion.1), calls=%async_computation.1 | async-start | bytes 4194304 | tf_op jit(solution)/shard_map/all_to_all | solution.py:124
  99.8 177.4 %all-gather.2.cloned.1.call-start = ((), (), s32[]{:S(2)}) async-start(), calls=%async_computation.3 | async-start | bytes 2359296 | tf_op jit(solution)/shard_map/all_gather | solution.py:86
  103.7 5.1 %copy-start.2 = (s32[1,1,2,35]{3,2,1,0:T(2,128)S(1)}, s32[1,1,2,35]{3,2,1,0:T(2,128)}, u32[]{:S(2)}) copy-start(s32[1,1,2,35]{3,2,1,0:T(2,128)} %param.10) | copy-start | bytes 844
  222.9 7.2 %copy-start.6 = (f32[1,31]{1,0:T(1,128)S(1)}, f32[1,31]{1,0:T(1,128)}, u32[]{:S(2)}) copy-start(f32[1,31]{1,0:T(1,128)} %param.15) | copy-start | bytes 376
  223.7 18.1 %copy-start.1 = (bf16[1024,128]{1,0:T(8,128)(2,1)S(1)}, bf16[1024,128]{1,0:T(8,128)(2,1)}, u32[]{:S(2)}) copy-start(bf16[1024,128]{1,0:T(8,128)(2,1)} %divide_convert_fusion) | copy-start | bytes 786436
  223.8 73.3 %reduce-scatter.2.cloned.1.call-start = ((), (), s32[]{:S(2)}) async-start(), calls=%async_computation.4 | async-start | bytes 655360 | tf_op jit(solution)/shard_map/reduce_scatter | solution.py:148
  225.3 14.3 %collective-permute-start = (bf16[1024,15]{1,0:T(8,128)(2,1)S(1)}, bf16[1024,15]{1,0:T(8,128)(2,1)S(1)}, u32[]{:S(2)}, u32[]{:S(2)}) collective-permute-start(bf16[1024,15]{1,0:T(8,128)(2,1)S(1)} %get-tuple-element.10), channel_id=1, source_target_pairs={{0,4},{4,8},{8,12},{12,16},{16,20},{20,24},{24,28},{28,0},{1,5},{5... | collective-permute-start | bytes 92168 | tf_op jit(solution)/shard_map/ppermute | solution.py:18
  226.9 15.0 %collective-permute-start.1 = (bf16[1024,15]{1,0:T(8,128)(2,1)S(1)}, bf16[1024,15]{1,0:T(8,128)(2,1)S(1)}, u32[]{:S(2)}, u32[]{:S(2)}) collective-permute-start(bf16[1024,15]{1,0:T(8,128)(2,1)S(1)} %get-tuple-element.11), channel_id=1, source_target_pairs={{4,0},{8,4},{12,8},{16,12},{20,16},{24,20},{28,24},{0,28},{5,1},{9... | collective-permute-start | bytes 92168 | tf_op jit(solution)/shard_map/ppermute | solution.py:21
Sparse Core Ops, SparseCore 0:
  223.9 53.1 all-gather.1
Sparse Core Ops, SparseCore 1:
  243.6 20.2 reduce-scatter.1
where the time goes:
time: 307 us; the launch traced here: 305 us
  local copies, waits for them, and re-layouts  102 us (33%)
  other arithmetic  57.9 us (19%)
  blocking collectives  53.7 us (17%)
  waiting for transfers between devices  40.8 us (13%)
  matrix products  22.3 us (7%)
  between operations  15.7 us (5%)
  starting transfers between devices  12.2 us (4%)
    all_to_all x1, blocking collectives, body(): lax.all_to_all(send_weight, 'sky', split_axis=1, concat_axis=1, tiled=True)  53.7 us
    unnamed x39, local copies, waits for them, and re-layouts  35.3 us
    eq x2, other arithmetic, keep_pixels(): return jnp.logical_and(row_bits[:, None] == 0, column_bits[None, :] == 0)  35.2 us
    all_gather x1, waiting for transfers between devices, subtract_template(): lax.all_gather(template, 'sky', axis=1, tiled=True)  29.6 us
    convert_element_type x1, local copies, waits for them, and re-layouts, psf_match(): column_pass.reshape(NB, side_length, side_length).astype(jnp.bfloat16)  24.6 us
    scatter x2, local copies, waits for them, and re-layouts, body(): empty_slots.at[:, own_columns, :]  11.4 us
    dot_general x1, matrix products, psf_match(): jnp.einsum('ikwx,kwt->itx', row_blocks, row_band, preferred_element_type=...  9.89 us
    dot_general x1, matrix products, psf_match(): jnp.einsum('jyw,kwt->kyjt', blocks, column_band, preferred_element_type=j...  9.18 us
  transfers between devices with their start and end apart: 5, of which 3 were waited for; matrix products, arithmetic and copies ran while one was open for 31% of the time, Pallas kernels for 0%

commit v1 on v0

--- a/solution.py
+++ b/solution.py
@@ -1,3 +1,4 @@
+import functools
 import jax
 import jax.numpy as jnp
 from jax import lax
@@ -7,6 +8,34 @@
 NB = 9
 TAPS = 25
 DTAPS = 31
+
+
+def draft_edges_here(my_data, d0, block_in):
+    m_next = my_data.shape
+    return jnp.moveaxis(
+        my_data.reshape(*m_next[:d0], block_in, m_next[d0] // block_in, *m_next[d0 + 1 :]), d0, 0
+    )
+
+
+def search_widths_for(page, join_dim):
+    block_out = list(page.shape[1:])
+    block_out[join_dim] *= page.shape[0]
+    return jnp.moveaxis(page, 0, join_dim).reshape(block_out)
+
+
+def convert_panels(s0, ax_name, here_x, chunk):
+    f_now, carry = (lax.axis_size(ax_name), lax.axis_index(ax_name))
+    outcome_arr = draft_edges_here(s0, here_x, f_now)
+    y2 = outcome_arr
+    for hop_no in range(1, f_now):
+        z_new, found_now = ((carry + hop_no) % f_now, (carry - hop_no) % f_now)
+        x_now = lax.dynamic_index_in_dim(outcome_arr, z_new, 0)
+        v_now = lax.ppermute(x_now, ax_name, [(d, (d + hop_no) % f_now) for d in range(f_now)])
+        y2 = lax.dynamic_update_slice_in_dim(y2, v_now, found_now, axis=0)
+    return search_widths_for(y2, chunk)
+
+
+settle_frames_on = functools.partial(convert_panels, ax_name="sky", here_x=1, chunk=1)
 
 
 def with_halo(block, sides, width):
@@ -122,7 +151,7 @@
     template = average_pieces(
         (
             lax.all_to_all(send_matched, "sky", split_axis=1, concat_axis=1, tiled=True),
-            lax.all_to_all(send_weight, "sky", split_axis=1, concat_axis=1, tiled=True),
+            settle_frames_on(send_weight),
         )
     )
     difference = subtract_template(template, matched, own_columns, side_length, sky_count)

time: 307 us -> 295 us (0.961)
  blocking collectives: 53.7 us -> 0 us
  starting transfers between devices: 12.2 us -> 39.7 us
  waiting for transfers between devices: 40.8 us -> 62.6 us
  local copies, waits for them, and re-layouts: 102 us -> 96.7 us
    all_to_all x1 -> x0, blocking collectives: 53.7 us -> none  [body(): lax.all_to_all(send_weight, 'sky', split_axis=1, concat_axis=1, tiled=True)]
    ppermute x0 -> x7, waiting for transfers between devices: none -> 20.6 us  [convert_panels(): lax.ppermute(x_now, ax_name, [(d, (d + hop_no) % f_now) for d in range(f_...]
    ppermute x0 -> x7, starting transfers between devices: none -> 15.7 us  [convert_panels(): lax.ppermute(x_now, ax_name, [(d, (d + hop_no) % f_now) for d in range(f_...]
    ppermute x1, starting transfers between devices: 3.26 us -> 12.1 us  [with_halo(): lax.ppermute(lax.slice_in_dim(block, 0, width, axis=dim), axis, backward)]
    ppermute x1, waiting for transfers between devices: 8.96 us -> 4.07 us  [with_halo(): lax.ppermute(lax.slice_in_dim(block, block.shape[dim] - width, None, axis...]
    gather x1 -> x0, other arithmetic: 4.55 us -> none  [keep_pixels(): planes[0][places // 30]]
    gather x29 -> x15, other arithmetic: 5.49 us -> 9.26 us  [keep_pixels(): planes[1][places // 30]]
    ppermute x1, waiting for transfers between devices: 2.2 us -> 5.9 us  [with_halo(): lax.ppermute(lax.slice_in_dim(block, 0, width, axis=dim), axis, backward)]
  transfers between devices with their start and end apart: 5 -> 12, of which waited for: 3 -> 7; matrix products, arithmetic and copies ran while one was open for 31% -> 30% of each run, Pallas kernels for 0% -> 0%
where the time goes in v1:
time: 295 us; the launch traced here: 293 us
  local copies, waits for them, and re-layouts  96.7 us (33%)
  waiting for transfers between devices  62.6 us (21%)
  other arithmetic  55.6 us (19%)
  starting transfers between devices  39.7 us (13%)
  matrix products  22.3 us (8%)
  between operations  16 us (5%)
    unnamed x45, local copies, waits for them, and re-layouts  35.2 us
    eq x2, other arithmetic, keep_pixels(): return jnp.logical_and(row_bits[:, None] == 0, column_bits[None, :] == 0)  35.2 us
    all_gather x1, waiting for transfers between devices, subtract_template(): lax.all_gather(template, 'sky', axis=1, tiled=True)  32 us
    convert_element_type x1, local copies, waits for them, and re-layouts, psf_match(): column_pass.reshape(NB, side_length, side_length).astype(jnp.bfloat16)  24.6 us
    ppermute x7, waiting for transfers between devices, convert_panels(): lax.ppermute(x_now, ax_name, [(d, (d + hop_no) % f_now) for d in range(f_...  20.6 us
    ppermute x7, starting transfers between devices, convert_panels(): lax.ppermute(x_now, ax_name, [(d, (d + hop_no) % f_now) for d in range(f_...  15.7 us
    ppermute x1, starting transfers between devices, with_halo(): lax.ppermute(lax.slice_in_dim(block, 0, width, axis=dim), axis, backward)  12.1 us
    dot_general x1, matrix products, psf_match(): jnp.einsum('ikwx,kwt->itx', row_blocks, row_band, preferred_element_type=...  9.89 us
  transfers between devices with their start and end apart: 12, of which 7 were waited for; matrix products, arithmetic and copies ran while one was open for 30% of the time, Pallas kernels for 0%

profile of v1, /device:TPU:0, one launch (start us, length us, event | category | flops | bytes accessed | tf_op | source)
XLA Modules:
  0.0 293.0 jit_solution(2320375371692488324)
XLA Ops:
  8.0 2.9 copy.65
  11.8 0.6 fusion.21
  12.4 9.2 %convolution_convert_fusion = bf16[9,128,8,1024]{3,1,2,0:T(8,128)(2,1)} fusion(bf16[8,1024,152]{1,2,0:T(8,128)(2,1)S(1)} %fusion.36, bf16[9,152,128,1]{2,0,1,3:T(8,128)(2,1)S(1)} %fusion.21), kind=kOutput, calls=%fused_computation.5 | convolution fusion | flops 2878341120 | bytes 21714944 | tf_op jit(solution)/shard_map/jyw,kwt->kyjt/dot_general | solution.py:89
  21.6 24.6 %copy.67 = bf16[9,1024,1024]{2,1,0:T(8,128)(2,1)} copy(bf16[9,1024,1024]{1,2,0:T(8,128)(2,1)} %bitcast.265) | data formatting | bytes 37748736 | tf_op jit(solution)/shard_map/convert_element_type | solution.py:92
  46.3 4.3 %fusion.4 = bf16[8,9,152,1024]{3,2,1,0:T(8,128)(2,1)} fusion(bf16[9,1024,1024]{2,1,0:T(8,128)(2,1)} %copy.67), kind=kLoop, calls=%fused_computation.15 | loop fusion | bytes 21676032
  50.6 3.8 %copy-done = bf16[9,1024,1024]{2,1,0:T(8,128)(2,1)S(1)} copy-done((bf16[9,1024,1024]{2,1,0:T(8,128)(2,1)S(1)}, bf16[9,1024,1024]{2,1,0:T(8,128)(2,1)}, u32[]{:S(2)}) %copy-start) | copy-done | bytes 18874392
  54.4 2.5 fusion.12
  56.9 2.4 fusion.11
  59.3 2.5 fusion.10
  61.8 2.5 fusion.9
  64.3 2.4 fusion.8
  66.7 2.4 fusion.7
  69.2 2.4 fusion.6
  71.6 0.6 fusion.22
  72.2 9.9 %bitcast_convert_fusion = bf16[128,8,1024]{2,0,1:T(8,128)(2,1)S(1)} fusion(bf16[8,9,152,1024]{3,2,1,0:T(8,128)(2,1)} %fusion.6, bf16[9,152,128]{2,0,1:T(8,128)(2,1)S(1)} %fusion.22), kind=kOutput, calls=%fused_computation.11 | convolution fusion | flops 2869952512 | bytes 24860672 | tf_op jit(solution)/shard_map/ikwx,kwt->itx/dot_general | solution.py:102
  82.1 1.3 copy-done.1
  83.4 0.6 copy.89
  84.3 0.7 fusion.63
  85.0 1.6 broadcast_in_dim.16.clone.1
  86.6 5.0 %scatter_fusion.1 = bf16[1024,8,128]{2,0,1:T(8,128)(2,1)} fusion(bf16[1024,8,128]{2,0,1:T(8,128)(2,1)} %broadcast_in_dim.16.clone.1, s32[8]{0:T(128)S(1)} %fusion.63, bf16[8,1024,128]{2,1,0:T(8,128)(2,1)S(1)} %bitcast.277), kind=kCustom, calls=%fused_computation.2 | custom fusion | bytes 6291488 | tf_op jit(solution)/shard_map/scatter | solution.py:145
  91.6 7.5 %all-to-all-start = ((bf16[1024,8,128]{2,0,1:T(8,128)(2,1)}), bf16[1024,8,128]{2,0,1:T(8,128)(2,1)}, u32[]{:S(2)}, u32[]{:S(2)}) async-start(bf16[1024,8,128]{2,0,1:T(8,128)(2,1)} %scatter_fusion.1), calls=%async_computation | async-start | bytes 4194304 | tf_op jit(solution)/shard_map/all_to_all | solution.py:153
  99.2 2.6 copy.75
  101.8 3.0 %copy.76 = bf16[1024,8,128]{2,0,1:T(8,128)(2,1)S(1)} copy(bf16[1024,8,128]{0,2,1:T(8,128)(2,1)} %bitcast.282) | data formatting | bytes 4194304 | tf_op jit(solution)/shard_map/squeeze | solution.py:141
  105.5 0.7 fusion.69
  106.2 0.7 fusion.66
  106.9 0.7 fusion.68
  107.6 0.7 fusion.67
  108.4 8.7 %compare_select_fusion.1 = (s32[1024,1]{0,1:T(1,128)S(1)}, s32[1024,1]{0,1:T(1,128)S(1)}) fusion(s32[]{:T(128)} %bitcast.63, s32[]{:T(128)} %bitcast.64, s32[]{:T(128)} %bitcast.65, s32[]{:T(128)} %bitcast.66, s32[]{:T(128)} %bitcast.67, s32[]{:T(128)} %bitcast.69, s32[]{:T(128)} %bitcast.68, s32[]{:T(128)} %bitcast.105, s32[]{:T(128)} %bitcast.104, ...), kind=kLoop, calls=%fused_computation.133 | loop fusion | flops 29696 | bytes 8248 | tf_op jit(solution)/shard_map/gather | solution.py:71
  117.0 17.6 %fusion.51 = pred[8,128]{1,0:T(8,128)(4,1)S(1)} fusion(pred[1024]{0:T(1024)(128)(4,1)S(1)} %get-tuple-element.87, pred[1024]{0:T(1024)(128)(4,1)S(1)} %get-tuple-element.88, pred[1024]{0:T(1024)(128)(4,1)S(1)} %get-tuple-element.89, pred[1024]{0:T(1024)(128)(4,1)S(1)} %get-tuple-element.90, pred[1024]{0:T(1024)(128)(4,1)S(1)} %get-tuple-element.91, ...), kind=kLoop, calls=%fused_computation.156 | loop fusion | flops 39936 | bytes 33904 | tf_op jit(solution)/shard_map/eq | solution.py:72
  134.6 17.6 %fusion.48 = pred[1024]{0:T(1024)(128)(4,1)S(1)} fusion(pred[1024]{0:T(1024)(128)(4,1)S(1)} %get-tuple-element.87, pred[1024]{0:T(1024)(128)(4,1)S(1)} %get-tuple-element.88, pred[1024]{0:T(1024)(128)(4,1)S(1)} %get-tuple-element.89, pred[1024]{0:T(1024)(128)(4,1)S(1)} %get-tuple-element.90, pred[1024]{0:T(1024)(128)(4,1)S(1)} %get-tuple-element.91, ...), kind=kLoop, calls=%fused_computation.153 | loop fusion | flops 37888 | bytes 33904 | tf_op jit(solution)/shard_map/eq | solution.py:72
  152.2 2.1 fusion.18
  154.6 3.3 %scatter_fusion = bf16[1024,8,128]{2,0,1:T(8,128)(2,1)S(1)} fusion(bf16[1024,8,128]{2,0,1:T(8,128)(2,1)S(1)} %broadcast_in_dim.16.clone, s32[8]{0:T(128)S(1)} %fusion.63, bf16[8,1024,128]{2,1,0:T(8,128)(2,1)} %fusion.18), kind=kCustom, calls=%fused_computation.1 | custom fusion | bytes 6291488 | tf_op jit(solution)/shard_map/scatter | solution.py:148
  157.9 1.3 dynamic-slice_bitcast_fusion
  159.3 1.9 collective-permute-start
  161.1 1.5 collective-permute-start.1
  162.6 2.4 collective-permute-start.2
  165.0 1.5 collective-permute-start.3
  166.4 2.4 collective-permute-start.4
  168.8 2.7 collective-permute-done
  171.5 1.7 collective-permute-start.5
  173.3 4.4 %collective-permute-start.6 = (bf16[1,1024,1,128]{3,1,0,2:T(8,128)(2,1)}, bf16[1,1024,1,128]{3,1,0,2:T(8,128)(2,1)S(1)}, u32[]{:S(2)}, u32[]{:S(2)}) collective-permute-start(bf16[1,1024,1,128]{3,1,0,2:T(8,128)(2,1)} %get-tuple-element.8), channel_id=1, source_target_pairs={{0,28},{4,0},{8,4},{12,8},{16,12},{20,16},{24,20},{28,24},{1,29},{... | collective-permute-start | bytes 786440 | tf_op jit(solution)/shard_map/ppermute | solution.py:33
  177.7 14.8 %collective-permute-done.2 = bf16[1,1024,1,128]{3,1,0,2:T(8,128)(2,1)S(1)} collective-permute-done((bf16[1,1024,1,128]{3,1,0,2:T(8,128)(2,1)}, bf16[1,1024,1,128]{3,1,0,2:T(8,128)(2,1)S(1)}, u32[]{:S(2)}, u32[]{:S(2)}) %collective-permute-start.2) | collective-permute-done | bytes 262176 | tf_op jit(solution)/shard_map/ppermute | solution.py:33
  192.6 0.4 collective-permute-done.3
  193.1 2.7 collective-permute-done.6
  196.1 2.2 fusion.2
  198.3 0.8 divide_convert_fusion
  199.2 0.3 iota_compare_fusion
  199.6 1.2 fusion.65
  200.7 4.4 %collective-permute-start.7 = (bf16[1024,15]{1,0:T(8,128)(2,1)S(1)}, bf16[1024,15]{1,0:T(8,128)(2,1)S(1)}, u32[]{:S(2)}, u32[]{:S(2)}) collective-permute-start(bf16[1024,15]{1,0:T(8,128)(2,1)S(1)} %get-tuple-element.15), channel_id=1, source_target_pairs={{0,4},{4,8},{8,12},{12,16},{16,20},{20,24},{24,28},{28,0},{1,5},{5... | collective-permute-start | bytes 92168 | tf_op jit(solution)/shard_map/ppermute | solution.py:47
  205.2 12.1 %collective-permute-start.8 = (bf16[1024,15]{1,0:T(8,128)(2,1)S(1)}, bf16[1024,15]{1,0:T(8,128)(2,1)S(1)}, u32[]{:S(2)}, u32[]{:S(2)}) collective-permute-start(bf16[1024,15]{1,0:T(8,128)(2,1)S(1)} %get-tuple-element.16), channel_id=1, source_target_pairs={{4,0},{8,4},{12,8},{16,12},{20,16},{24,20},{28,24},{0,28},{5,1},{9... | collective-permute-start | bytes 92168 | tf_op jit(solution)/shard_map/ppermute | solution.py:50
  217.2 0.5 fusion.13
  217.8 4.1 %collective-permute-done.7 = bf16[1024,15]{1,0:T(8,128)(2,1)S(1)} collective-permute-done((bf16[1024,15]{1,0:T(8,128)(2,1)S(1)}, bf16[1024,15]{1,0:T(8,128)(2,1)S(1)}, u32[]{:S(2)}, u32[]{:S(2)}) %collective-permute-start.7) | collective-permute-done | bytes 30752 | tf_op jit(solution)/shard_map/ppermute | solution.py:47
  221.9 5.9 %collective-permute-done.8 = bf16[1024,15]{1,0:T(8,128)(2,1)S(1)} collective-permute-done((bf16[1024,15]{1,0:T(8,128)(2,1)S(1)}, bf16[1024,15]{1,0:T(8,128)(2,1)S(1)}, u32[]{:S(2)}, u32[]{:S(2)}) %collective-permute-start.8) | collective-permute-done | bytes 30752 | tf_op jit(solution)/shard_map/ppermute | solution.py:50
  227.8 0.4 convolution_convert_fusion.1
  228.4 1.1 convolution_multiply_fusion
  229.5 3.2 %copy.81 = f32[1,1,1024,1024]{2,3,1,0:T(8,128)} copy(bf16[1,1,1024,1024]{3,2,1,0:T(8,128)(2,1)S(1)} %bitcast.276) | data formatting | bytes 6291456 | tf_op jit(solution)/shard_map/convert_element_type | solution.py:119
  232.7 0.7 compare_and_fusion
  233.5 32.0 %all-gather.2.cloned.1.call-done = bf16[1024,1024]{1,0:T(8,128)(2,1)} async-done(((bf16[1024,128]{1,0:T(8,128)(2,1)}), bf16[1024,1024]{1,0:T(8,128)(2,1)}) %all-gather.2.cloned.1.call-update) | async-done | bytes 2097168 | tf_op jit(solution)/shard_map/all_gather | solution.py:115
  265.5 3.9 %copy.78 = bf16[1024,1024]{0,1:T(8,128)(2,1)} copy(bf16[1024,1024]{1,0:T(8,128)(2,1)} %all-gather.2.cloned.1.call-done) | data formatting | bytes 4194304 | tf_op jit(solution)/shard_map/all_gather | solution.py:115
  269.5 3.0 %copy.79 = bf16[1024,8,128]{2,0,1:T(8,128)(2,1)S(1)} copy(bf16[1024,8,128]{0,2,1:T(8,128)(2,1)} %bitcast.280) | data formatting | bytes 4194304 | tf_op jit(solution)/shard_map/reshape | solution.py:115
  272.5 2.1 gather_fusion
  274.6 2.9 copy.80
  277.5 4.1 %subtract_convert_fusion = bf16[1,1,1024,1024]{2,3,1,0:T(8,128)(2,1)} fusion(f32[1,1,1024,1024]{2,3,1,0:T(8,128)} %copy.81, bf16[1,1,1024,1024]{2,3,1,0:T(8,128)(2,1)S(1)} %bitcast.278, pred[1024]{0:T(1024)(128)(4,1)S(1)} %broadcast_bitcast_fusion), kind=kLoop, calls=%fused_computation.12 | loop fusion | flops 4194304 | bytes 8389632 | tf_op jit(solution)/shard_map/convert_element_type | solution.py:119
  281.6 3.9 %copy.82 = bf16[1,1,1024,1024]{3,2,1,0:T(8,128)(2,1)} copy(bf16[1,1,1024,1024]{2,3,1,0:T(8,128)(2,1)} %subtract_convert_fusion) | data formatting | bytes 4194304
  (71 shorter events, 3.0 us)
Async XLA Ops:
  11.1 0.7 copy-start.6
  11.1 0.7 copy-start.7
  46.3 8.2 %copy-start = (bf16[9,1024,1024]{2,1,0:T(8,128)(2,1)S(1)}, bf16[9,1024,1024]{2,1,0:T(8,128)(2,1)}, u32[]{:S(2)}) copy-start(bf16[9,1024,1024]{2,1,0:T(8,128)(2,1)} %copy.67) | copy-start | bytes 56623108
  69.2 2.4 copy-start.8
  82.1 1.3 copy-start.1
  91.6 7.6 %copy-start.4 = (bf16[1,1,1024,1024]{3,2,1,0:T(8,128)(2,1)S(1)}, bf16[1,1,1024,1024]{3,2,1,0:T(8,128)(2,1)}, u32[]{:S(2)}) copy-start(bf16[1,1,1024,1024]{3,2,1,0:T(8,128)(2,1)} %param.9) | copy-start | bytes 6291460
  91.6 104.5 %all-to-all-start = ((bf16[1024,8,128]{2,0,1:T(8,128)(2,1)}), bf16[1024,8,128]{2,0,1:T(8,128)(2,1)}, u32[]{:S(2)}, u32[]{:S(2)}) async-start(bf16[1024,8,128]{2,0,1:T(8,128)(2,1)} %scatter_fusion.1), calls=%async_computation | async-start | bytes 4194304 | tf_op jit(solution)/shard_map/all_to_all | solution.py:153
  99.1 166.5 %all-gather.2.cloned.1.call-start = ((), (), s32[]{:S(2)}) async-start(), calls=%async_computation.2 | async-start | bytes 2359296 | tf_op jit(solution)/shard_map/all_gather | solution.py:115
  101.8 3.7 %copy-start.5 = (s32[1,1,2,35]{3,2,1,0:T(2,128)S(1)}, s32[1,1,2,35]{3,2,1,0:T(2,128)}, u32[]{:S(2)}) copy-start(s32[1,1,2,35]{3,2,1,0:T(2,128)} %param.10) | copy-start | bytes 844
  159.3 12.3 %collective-permute-start = (bf16[1,1024,1,128]{3,1,0,2:T(8,128)(2,1)}, bf16[1,1024,1,128]{3,1,0,2:T(8,128)(2,1)S(1)}, u32[]{:S(2)}, u32[]{:S(2)}) collective-permute-start(bf16[1,1024,1,128]{3,1,0,2:T(8,128)(2,1)} %get-tuple-element.14), channel_id=1, source_target_pairs={{0,4},{4,8},{8,12},{12,16},{16,20},{20,24},{24,28},{28,0},{1,5},{5... | collective-permute-start | bytes 786440 | tf_op jit(solution)/shard_map/ppermute | solution.py:33
  161.1 12.1 %collective-permute-start.1 = (bf16[1,1024,1,128]{3,1,0,2:T(8,128)(2,1)}, bf16[1,1024,1,128]{3,1,0,2:T(8,128)(2,1)S(1)}, u32[]{:S(2)}, u32[]{:S(2)}) collective-permute-start(bf16[1,1024,1,128]{3,1,0,2:T(8,128)(2,1)} %get-tuple-element.13), channel_id=1, source_target_pairs={{0,8},{4,12},{8,16},{12,20},{16,24},{20,28},{24,0},{28,4},{1,9},{5... | collective-permute-start | bytes 786440 | tf_op jit(solution)/shard_map/ppermute | solution.py:33
  162.6 29.9 %collective-permute-start.2 = (bf16[1,1024,1,128]{3,1,0,2:T(8,128)(2,1)}, bf16[1,1024,1,128]{3,1,0,2:T(8,128)(2,1)S(1)}, u32[]{:S(2)}, u32[]{:S(2)}) collective-permute-start(bf16[1,1024,1,128]{3,1,0,2:T(8,128)(2,1)} %get-tuple-element.12), channel_id=1, source_target_pairs={{0,12},{4,16},{8,20},{12,24},{16,28},{20,0},{24,4},{28,8},{1,13},{... | collective-permute-start | bytes 786440 | tf_op jit(solution)/shard_map/ppermute | solution.py:33
  165.0 28.0 %collective-permute-start.3 = (bf16[1,1024,1,128]{3,1,0,2:T(8,128)(2,1)}, bf16[1,1024,1,128]{3,1,0,2:T(8,128)(2,1)S(1)}, u32[]{:S(2)}, u32[]{:S(2)}) collective-permute-start(bf16[1,1024,1,128]{3,1,0,2:T(8,128)(2,1)} %get-tuple-element.11), channel_id=1, source_target_pairs={{0,16},{4,20},{8,24},{12,28},{16,0},{20,4},{24,8},{28,12},{1,17},{... | collective-permute-start | bytes 786440 | tf_op jit(solution)/shard_map/ppermute | solution.py:33
  166.4 26.6 %collective-permute-start.4 = (bf16[1,1024,1,128]{3,1,0,2:T(8,128)(2,1)}, bf16[1,1024,1,128]{3,1,0,2:T(8,128)(2,1)S(1)}, u32[]{:S(2)}, u32[]{:S(2)}) collective-permute-start(bf16[1,1024,1,128]{3,1,0,2:T(8,128)(2,1)} %get-tuple-element.10), channel_id=1, source_target_pairs={{0,20},{4,24},{8,28},{12,0},{16,4},{20,8},{24,12},{28,16},{1,21},{... | collective-permute-start | bytes 786440 | tf_op jit(solution)/shard_map/ppermute | solution.py:33
  171.5 21.5 %collective-permute-start.5 = (bf16[1,1024,1,128]{3,1,0,2:T(8,128)(2,1)}, bf16[1,1024,1,128]{3,1,0,2:T(8,128)(2,1)S(1)}, u32[]{:S(2)}, u32[]{:S(2)}) collective-permute-start(bf16[1,1024,1,128]{3,1,0,2:T(8,128)(2,1)} %get-tuple-element.9), channel_id=1, source_target_pairs={{0,24},{4,28},{8,0},{12,4},{16,8},{20,12},{24,16},{28,20},{1,25},{... | collective-permute-start | bytes 786440 | tf_op jit(solution)/shard_map/ppermute | solution.py:33
  173.3 22.5 %collective-permute-start.6 = (bf16[1,1024,1,128]{3,1,0,2:T(8,128)(2,1)}, bf16[1,1024,1,128]{3,1,0,2:T(8,128)(2,1)S(1)}, u32[]{:S(2)}, u32[]{:S(2)}) collective-permute-start(bf16[1,1024,1,128]{3,1,0,2:T(8,128)(2,1)} %get-tuple-element.8), channel_id=1, source_target_pairs={{0,28},{4,0},{8,4},{12,8},{16,12},{20,16},{24,20},{28,24},{1,29},{... | collective-permute-start | bytes 786440 | tf_op jit(solution)/shard_map/ppermute | solution.py:33
  198.3 18.9 %copy-start.9 = (f32[1,31]{1,0:T(1,128)S(1)}, f32[1,31]{1,0:T(1,128)}, u32[]{:S(2)}) copy-start(f32[1,31]{1,0:T(1,128)} %param.15) | copy-start | bytes 376
  199.1 28.6 %copy-start.3 = (bf16[1024,128]{1,0:T(8,128)(2,1)S(1)}, bf16[1024,128]{1,0:T(8,128)(2,1)}, u32[]{:S(2)}) copy-start(bf16[1024,128]{1,0:T(8,128)(2,1)} %divide_convert_fusion) | copy-start | bytes 786436
  199.2 86.4 %reduce-scatter.2.cloned.1.call-start = ((), (), s32[]{:S(2)}) async-start(), calls=%async_computation.3 | async-start | bytes 655360 | tf_op jit(solution)/shard_map/reduce_scatter | solution.py:177
  200.7 21.1 %collective-permute-start.7 = (bf16[1024,15]{1,0:T(8,128)(2,1)S(1)}, bf16[1024,15]{1,0:T(8,128)(2,1)S(1)}, u32[]{:S(2)}, u32[]{:S(2)}) collective-permute-start(bf16[1024,15]{1,0:T(8,128)(2,1)S(1)} %get-tuple-element.15), channel_id=1, source_target_pairs={{0,4},{4,8},{8,12},{12,16},{16,20},{20,24},{24,28},{28,0},{1,5},{5... | collective-permute-start | bytes 92168 | tf_op jit(solution)/shard_map/ppermute | solution.py:47
  205.2 22.6 %collective-permute-start.8 = (bf16[1024,15]{1,0:T(8,128)(2,1)S(1)}, bf16[1024,15]{1,0:T(8,128)(2,1)S(1)}, u32[]{:S(2)}, u32[]{:S(2)}) collective-permute-start(bf16[1024,15]{1,0:T(8,128)(2,1)S(1)} %get-tuple-element.16), channel_id=1, source_target_pairs={{4,0},{8,4},{12,8},{16,12},{20,16},{24,20},{28,24},{0,28},{5,1},{9... | collective-permute-start | bytes 92168 | tf_op jit(solution)/shard_map/ppermute | solution.py:50
  217.8 11.7 %copy-start.2 = (bf16[128,8,1024]{2,0,1:T(8,128)(2,1)S(1)}, bf16[128,8,1024]{2,0,1:T(8,128)(2,1)}, u32[]{:S(2)}) copy-start(bf16[128,8,1024]{2,0,1:T(8,128)(2,1)} %copy-done.1) | copy-start | bytes 6291460
Sparse Core Ops, SparseCore 0:
  199.3 66.2 all-gather.1
Sparse Core Ops, SparseCore 1:
  229.6 23.4 reduce-scatter.1
